TPU v7x, 256 devices: a whole 4x4x8 slice. The times are simulated.
256 devices in a mesh: tc: 128 (over z, x, y), pr: 2 (over core).
Axes of the slice: x: 4, y: 4, z: 8, core: 2. Of those that a mesh axis runs over, the one named last changes fastest.
Arguments:
- pivot_rhs: float32 [128, 1536, 64], P('tc', None, 'pr'), may hold values from -6 to 6
- pivot_inverse: bfloat16 [128, 1536, 1536], P('tc'), as said below
- pivot_owner: int32 [3], replicated, may hold values from 0 to 127, as said below
- coupling_left: bfloat16 [128, 2, 1536, 200], P('tc'), may hold values from -0.15625 to 0.15625
- coupling_right: bfloat16 [128, 2, 1536, 200], P('tc'), may hold values from -0.4375 to 0.4375
- coupling_ranks: int32 [128, 2], P('tc'), may hold values from 100 to 200, as said below
- future_left: bfloat16 [256, 3, 200, 1536], P('tc', None, None, 'pr'), may hold values from -0.15625 to 0.15625
- future_right: bfloat16 [256, 3, 200, 1536], P('tc', None, None, 'pr'), may hold values from -0.4375 to 0.4375
- future_ranks: int32 [256, 3], P('tc'), may hold values from 100 to 200, as said below
- future_rhs: float32 [256, 64, 1536], P('tc', None, 'pr'), may hold values from -6 to 6
Outputs:
- solved: bfloat16 [3, 1536, 64], P(None, None, 'pr')
- future_out: float32 [256, 64, 1536], P('tc', None, 'pr')
Inputs may be any that keep to these rules, and one draw needn't show every extreme that they name: `pivot_owner`: the 3 entries are distinct; entry p names the slot, and so the index of tc, that holds pivot p's tiles. `coupling_ranks`: entry [s, j] is the rank of the tile from the pivot in slot s to the pivot j + 1 places later. In every draw a tile that the window uses has rank exactly 200. `future_ranks`: in every draw one of these tiles has rank exactly 200. `pivot_inverse`: each tile is lower triangular.
All inputs are finite; a program needn't handle non-finite values.
Results may differ from a plain program's by a relative error of at most 0.007.
Values may be sent and summed in bfloat16 or wider, within the bound.
A program may use at most 64 MiB of HBM per device.

v0:
```python
import jax
import jax.numpy as jnp
from jax import lax
from jax.sharding import Mesh
from jax.sharding import PartitionSpec as P

TC = ("tc_0", "tc_1", "tc_2")


def padded_to(lines, count):
    spare = -lines.shape[0] % count
    if not spare:
        return lines
    return jnp.concatenate([lines, jnp.zeros((spare, *lines.shape[1:]), lines.dtype)])


def sent_to_all(shard, axis):
    count = lax.axis_size(axis)
    return lax.all_to_all(
        jnp.broadcast_to(shard[None], (count, *shard.shape)), axis, 0, 0, tiled=True
    )


def in_order(pieces, dim):
    pieces = jnp.moveaxis(pieces, 0, dim)
    shape = pieces.shape
    return pieces.reshape(*shape[:dim], shape[dim] * shape[dim + 1], *shape[dim + 2 :])


def gathered_by_axis(shard, axes, dim):
    far, near = axes
    pieces = sent_to_all(sent_to_all(shard, far), near)
    return in_order(pieces.swapaxes(0, 1).reshape(-1, *shard.shape), dim)


def in_blocks(shard, dim, count):
    shape = shard.shape
    pieces = shard.reshape(*shape[:dim], count, shape[dim] // count, *shape[dim + 1 :])
    return jnp.moveaxis(pieces, dim, 0)


def sum_at_owner(shard, axis, dim):
    pieces = in_blocks(shard, dim, lax.axis_size(axis))
    arrived = lax.all_to_all(pieces, axis, split_axis=0, concat_axis=0, tiled=True)
    return arrived.sum(axis=0)


def summed_rows(shard, axes, dim):
    far, near = axes
    own = sum_at_owner(in_blocks(shard, dim, lax.axis_size(far)), near, dim + 1)
    return jnp.sum(lax.all_to_all(own, far, 0, 0, tiled=True), axis=0)


def nested_sum(shard, axes):
    lines = shard.reshape(-1, shard.shape[-1])
    padded = padded_to(lines, lax.axis_size(axes[0]) * lax.axis_size(axes[1]))
    whole = gathered_by_axis(summed_rows(padded, axes, 0), axes, 0)
    return lax.slice_in_dim(whole, 0, len(lines)).reshape(shard.shape)


def over_copies(shard, axis):
    return sent_to_all(shard, axis).sum(axis=0)


def apply_weights(products, right_part, ranks_part):
    rank_ids = lax.broadcasted_iota(jnp.int32, products.shape, 3)
    weights = jnp.where(rank_ids < ranks_part[:, :, None, None], products, 0.0).astype(jnp.bfloat16)
    return jnp.einsum("fsqr,fsrb->fqb", weights, right_part, preferred_element_type=jnp.float32)


def local(
    pivot_rhs,
    pivot_inverse,
    pivot_owner,
    coupling_left,
    coupling_right,
    coupling_ranks,
    future_left,
    future_right,
    future_ranks,
    future_rhs,
):
    tile_count = pivot_owner.shape[0]
    rank_width = coupling_left.shape[3]
    device_index = lax.axis_index(TC)
    owned_flags = pivot_owner == device_index
    holds_pivot = jnp.any(owned_flags)
    own_pivot = jnp.sum(jnp.where(owned_flags, jnp.arange(tile_count, dtype=jnp.int32), 0))
    pending = pivot_rhs[0]
    inverse_tile = pivot_inverse[0]
    rank_ids = lax.broadcasted_iota(jnp.int32, (rank_width, 1), 0)
    solved = [None] * tile_count
    future_acc = future_rhs
    for current in reversed(range(tile_count)):
        pivot_in = pending.astype(jnp.bfloat16)
        local_solution = lax.dot_general(
            inverse_tile, pivot_in, (((0,), (0,)), ((), ())), preferred_element_type=jnp.float32
        ).astype(jnp.bfloat16)
        is_root = device_index == pivot_owner[current]
        masked_block = jnp.where(is_root, local_solution.astype(jnp.float32), 0.0)
        solved_block = nested_sum(masked_block, (("tc_0", "tc_1"), "tc_2")).astype(jnp.bfloat16)
        solved[current] = solved_block
        if current > 0:
            distance = current - own_pivot - 1
            active = jnp.logical_and(holds_pivot, distance >= 0)
            slot_entry = jnp.clip(distance, 0, tile_count - 2)
            left_tile = lax.dynamic_index_in_dim(coupling_left[0], slot_entry, 0, keepdims=False)
            right_tile = lax.dynamic_index_in_dim(coupling_right[0], slot_entry, 0, keepdims=False)
            rank_limit = lax.dynamic_index_in_dim(coupling_ranks[0], slot_entry, 0, keepdims=False)
            factor = lax.dot_general(
                left_tile,
                solved_block,
                (((0,), (0,)), ((), ())),
                preferred_element_type=jnp.float32,
            )
            factor = jnp.where(rank_ids < rank_limit, factor, 0.0).astype(jnp.bfloat16)
            change = jnp.dot(right_tile, factor, preferred_element_type=jnp.float32)
            pending = pending - jnp.where(active, change, 0.0)
    stacked = jnp.stack(solved)
    columns = lax.all_to_all(stacked, "pr", split_axis=1, concat_axis=2, tiled=True)
    products = jnp.einsum(
        "sbq,fsrb->fsqr", columns, future_left, preferred_element_type=jnp.float32
    )
    products = over_copies(products, "pr")
    future_acc = future_acc - apply_weights(products, future_right, future_ranks)
    return (stacked, future_acc)


def solution(mesh):
    finer = Mesh(mesh.devices.reshape(8, 4, 4, mesh.shape["pr"]), ("tc_0", "tc_1", "tc_2", "pr"))
    in_specs = (
        P(TC, None, "pr"),
        P(TC, None, None),
        P(),
        P(TC, None, None, None),
        P(TC, None, None, None),
        P(TC, None),
        P(TC, None, None, "pr"),
        P(TC, None, None, "pr"),
        P(TC, None),
        P(TC, None, "pr"),
    )
    out_specs = (P(None, None, "pr"), P(TC, None, "pr"))
    return jax.shard_map(local, mesh=finer, in_specs=in_specs, out_specs=out_specs, check_vma=False)
```

profile of v0, /device:TPU:1, one launch (start us, length us, event | category | flops | bytes accessed | tf_op | source)
XLA Modules:
  0.0 229.7 jit_solution(5553572700771871744)
XLA Ops:
  0.7 1.4 fusion.79
  2.7 3.3 %fusion.15 = f32[1536,32]{0,1:T(8,128)S(1)} fusion(bf16[1,1536,1536]{2,1,0:T(8,128)(2,1)} %param.11, f32[1,1536,32]{1,2,0:T(8,128)} %param.10, pred[]{:T(512)S(6)} %eq.18), kind=kOutput, calls=%fused_computation.13 | convolution fusion | flops 151191552 | bytes 5111809 | tf_op jit(solution)/shard_map/dot_general | solution.py:96
  6.1 1.2 copy.102
  7.2 1.2 reshape_reshape.12
  8.4 1.3 copy.139
  9.8 1.5 reshape.72
  11.3 10.0 %all_to_all.83 = f32[4,1,12288]{2,1,0:T(1,128)S(1)} all-to-all(f32[4,1,12288]{2,1,0:T(1,128)S(1)} %reshape.72), channel_id=1, replica_groups=mesh['tc_0'=8,'tc_1'=4,'tc_2'=4,'pr'=2] {'tc_2'}, dimensions={0} | all-to-all | bytes 393216 | tf_op jit(solution)/shard_map/all_to_all | solution.py:44
  21.8 1.1 reduce
  24.1 11.0 %all-to-all-start.1 = ((f32[32,1,384]{2,1,0:T(1,128)}), f32[32,1,384]{2,1,0:T(1,128)S(1)}, u32[]{:S(2)}, u32[]{:S(2)}) async-start(f32[32,1,384]{2,1,0:T(1,128)} %reshape.74), calls=%async_computation.1 | async-start | bytes 98304 | tf_op jit(solution)/shard_map/all_to_all | solution.py:51
  35.9 8.0 %all-to-all-done.1 = f32[32,1,384]{2,1,0:T(1,128)S(1)} async-done(((f32[32,1,384]{2,1,0:T(1,128)}), f32[32,1,384]{2,1,0:T(1,128)S(1)}, u32[]{:S(2)}, u32[]{:S(2)}) %all-to-all-start.1) | async-done | bytes 49184 | tf_op jit(solution)/shard_map/all_to_all | solution.py:51
  45.5 3.9 %all-to-all-start.2 = ((bf16[32,2,192]{2,1,0:T(2,128)(2,1)}), bf16[32,2,192]{2,1,0:T(2,128)(2,1)S(1)}, u32[]{:S(2)}, u32[]{:S(2)}) async-start(bf16[32,2,192]{2,1,0:T(2,128)(2,1)} %reshape.76), calls=%async_computation.2 | async-start | bytes 65536 | tf_op jit(solution)/shard_map/all_to_all | solution.py:19
  53.2 4.8 %all-to-all-done.2 = bf16[32,2,192]{2,1,0:T(2,128)(2,1)S(1)} async-done(((bf16[32,2,192]{2,1,0:T(2,128)(2,1)}), bf16[32,2,192]{2,1,0:T(2,128)(2,1)S(1)}, u32[]{:S(2)}, u32[]{:S(2)}) %all-to-all-start.2) | async-done | bytes 24608 | tf_op jit(solution)/shard_map/all_to_all | solution.py:19
  59.3 3.3 %all-to-all-start.3 = ((bf16[4,2,6144]{2,1,0:T(2,128)(2,1)}), bf16[4,2,6144]{2,1,0:T(2,128)(2,1)S(1)}, u32[]{:S(2)}, u32[]{:S(2)}) async-start(bf16[4,2,6144]{2,1,0:T(2,128)(2,1)} %reshape.78), calls=%async_computation.3 | async-start | bytes 196608 | tf_op jit(solution)/shard_map/all_to_all | solution.py:19
  63.3 3.9 %all-to-all-done.3 = bf16[4,2,6144]{2,1,0:T(2,128)(2,1)S(1)} async-done(((bf16[4,2,6144]{2,1,0:T(2,128)(2,1)}), bf16[4,2,6144]{2,1,0:T(2,128)(2,1)S(1)}, u32[]{:S(2)}, u32[]{:S(2)}) %all-to-all-start.3) | async-done | bytes 98336 | tf_op jit(solution)/shard_map/all_to_all | solution.py:19
  67.9 1.9 fusion.6
  69.8 3.3 %fusion.27 = f32[1536,32]{0,1:T(8,128)S(1)} fusion(bf16[1,1536,1536]{2,1,0:T(8,128)(2,1)} %param.11, f32[1536,32]{0,1:T(8,128)S(1)} %fusion.6, pred[]{:T(512)S(6)} %eq.19), kind=kOutput, calls=%fused_computation.17 | convolution fusion | flops 151191552 | bytes 5111809 | tf_op jit(solution)/shard_map/dot_general | solution.py:96
  73.1 1.2 copy.107
  74.3 1.2 reshape_reshape.13
  75.5 1.3 copy.138
  76.8 1.5 reshape.80
  78.3 7.5 %all_to_all.84 = f32[4,1,12288]{2,1,0:T(1,128)S(1)} all-to-all(f32[4,1,12288]{2,1,0:T(1,128)S(1)} %reshape.80), channel_id=1, replica_groups=mesh['tc_0'=8,'tc_1'=4,'tc_2'=4,'pr'=2] {'tc_2'}, dimensions={0} | all-to-all | bytes 393216 | tf_op jit(solution)/shard_map/all_to_all | solution.py:44
  85.8 1.1 reduce.2
  87.6 12.9 %all_to_all.85 = f32[32,1,384]{2,1,0:T(1,128)S(1)} all-to-all(f32[32,1,384]{2,1,0:T(1,128)S(1)} %reshape.82), channel_id=1, replica_groups=mesh['tc_0'=8,'tc_1'=4,'tc_2'=4,'pr'=2] {'tc_0','tc_1'}, dimensions={0} | all-to-all | bytes 98304 | tf_op jit(solution)/shard_map/all_to_all | solution.py:51
  102.2 3.9 %all-to-all-start.6 = ((bf16[32,2,192]{2,1,0:T(2,128)(2,1)}), bf16[32,2,192]{2,1,0:T(2,128)(2,1)S(1)}, u32[]{:S(2)}, u32[]{:S(2)}) async-start(bf16[32,2,192]{2,1,0:T(2,128)(2,1)} %reshape.84), calls=%async_computation.6 | async-start | bytes 65536 | tf_op jit(solution)/shard_map/all_to_all | solution.py:19
  107.2 7.4 %all-to-all-done.6 = bf16[32,2,192]{2,1,0:T(2,128)(2,1)S(1)} async-done(((bf16[32,2,192]{2,1,0:T(2,128)(2,1)}), bf16[32,2,192]{2,1,0:T(2,128)(2,1)S(1)}, u32[]{:S(2)}, u32[]{:S(2)}) %all-to-all-start.6) | async-done | bytes 24608 | tf_op jit(solution)/shard_map/all_to_all | solution.py:19
  115.9 3.5 %all-to-all-start.7 = ((bf16[4,2,6144]{2,1,0:T(2,128)(2,1)}), bf16[4,2,6144]{2,1,0:T(2,128)(2,1)S(1)}, u32[]{:S(2)}, u32[]{:S(2)}) async-start(bf16[4,2,6144]{2,1,0:T(2,128)(2,1)} %reshape.86), calls=%async_computation.7 | async-start | bytes 196608 | tf_op jit(solution)/shard_map/all_to_all | solution.py:19
  120.1 3.7 %all-to-all-done.7 = bf16[4,2,6144]{2,1,0:T(2,128)(2,1)S(1)} async-done(((bf16[4,2,6144]{2,1,0:T(2,128)(2,1)}), bf16[4,2,6144]{2,1,0:T(2,128)(2,1)S(1)}, u32[]{:S(2)}, u32[]{:S(2)}) %all-to-all-start.7) | async-done | bytes 98336 | tf_op jit(solution)/shard_map/all_to_all | solution.py:19
  124.5 2.6 %fusion.8 = bf16[1536,32]{0,1:T(8,128)(2,1)} fusion(f32[1536,32]{0,1:T(8,128)S(1)} %copy-done.2, bf16[1536,32]{1,0:T(8,128)(2,1)S(1)} %convert_element_type.112, bf16[1,2,1536,200]{2,3,1,0:T(8,128)(2,1)} %param.13, s32[]{:T(128)S(6)} %min.8, bf16[1,2,1536,200]{2,3,1,0:T(8,128)(2,1)} %param.14, pred[]{:T(512)S(6)} %and.10, ...), kind=kOutput, calls=%fused_computation.10 | convolution fusion | flops 39481856 | bytes 1623752 | tf_op jit(solution)/shard_map/dot_general | solution.py:117
  127.0 3.3 %fusion.39 = f32[1536,32]{0,1:T(8,128)S(1)} fusion(bf16[1536,32]{0,1:T(8,128)(2,1)} %fusion.8, bf16[1,1536,1536]{2,1,0:T(8,128)(2,1)} %param.11, pred[]{:T(512)S(6)} %eq.15), kind=kOutput, calls=%fused_computation.21 | convolution fusion | flops 151142400 | bytes 5013505 | tf_op jit(solution)/shard_map/dot_general | solution.py:96
  130.3 1.2 copy.112
  131.6 2.2 reshape_reshape.14
  133.7 2.6 %copy.137 = f32[4,32,12,32]{3,1,2,0:T(8,128)} copy(f32[4,32,12,32]{3,2,0,1:T(8,128)} %bitcast.126) | data formatting | bytes 393216 | tf_op jit(solution)/shard_map/transpose | solution.py:39
  136.3 1.5 reshape.88
  137.8 7.5 %all_to_all.86 = f32[4,1,12288]{2,1,0:T(1,128)S(1)} all-to-all(f32[4,1,12288]{2,1,0:T(1,128)S(1)} %reshape.88), channel_id=1, replica_groups=mesh['tc_0'=8,'tc_1'=4,'tc_2'=4,'pr'=2] {'tc_2'}, dimensions={0} | all-to-all | bytes 393216 | tf_op jit(solution)/shard_map/all_to_all | solution.py:44
  146.5 1.2 reshape.89
  147.7 1.2 bitcast_reduce_fusion
  149.2 11.7 %all_to_all.87 = f32[32,1,384]{2,1,0:T(1,128)S(1)} all-to-all(f32[32,1,384]{2,1,0:T(1,128)S(1)} %reshape.90), channel_id=1, replica_groups=mesh['tc_0'=8,'tc_1'=4,'tc_2'=4,'pr'=2] {'tc_0','tc_1'}, dimensions={0} | all-to-all | bytes 98304 | tf_op jit(solution)/shard_map/all_to_all | solution.py:51
  161.9 11.6 %all_to_all.88 = bf16[32,2,192]{2,1,0:T(2,128)(2,1)S(1)} all-to-all(bf16[32,2,192]{2,1,0:T(2,128)(2,1)S(1)} %reshape.92), channel_id=1, replica_groups=mesh['tc_0'=8,'tc_1'=4,'tc_2'=4,'pr'=2] {'tc_0','tc_1'}, dimensions={0} | all-to-all | bytes 49152 | tf_op jit(solution)/shard_map/all_to_all | solution.py:19
  174.8 3.3 %all-to-all-start.11 = ((bf16[4,2,6144]{2,1,0:T(2,128)(2,1)}), bf16[4,2,6144]{2,1,0:T(2,128)(2,1)S(1)}, u32[]{:S(2)}, u32[]{:S(2)}) async-start(bf16[4,2,6144]{2,1,0:T(2,128)(2,1)} %reshape.94), calls=%async_computation.11 | async-start | bytes 196608 | tf_op jit(solution)/shard_map/all_to_all | solution.py:19
  179.2 3.8 %all-to-all-done.11 = bf16[4,2,6144]{2,1,0:T(2,128)(2,1)S(1)} async-done(((bf16[4,2,6144]{2,1,0:T(2,128)(2,1)}), bf16[4,2,6144]{2,1,0:T(2,128)(2,1)S(1)}, u32[]{:S(2)}, u32[]{:S(2)}) %all-to-all-start.11) | async-done | bytes 98336 | tf_op jit(solution)/shard_map/all_to_all | solution.py:19
  187.6 8.2 %copy.136 = bf16[3,1536,32]{2,0,1:T(4,128)(2,1)} copy(bf16[3,1536,32]{2,1,0:T(8,128)(2,1)S(1)} %constant_dynamic-update-slice_fusion) | data formatting | bytes 589824 | tf_op jit(solution)/shard_map/stack | solution.py:119
  195.8 2.3 reshape.96
  198.1 18.6 %all_to_all.89 = bf16[2,2,36864]{2,1,0:T(2,128)(2,1)} all-to-all(bf16[2,2,36864]{2,1,0:T(2,128)(2,1)S(1)} %reshape.96), channel_id=1, replica_groups=mesh['tc_0'=8,'tc_1'=4,'tc_2'=4,'pr'=2] {'pr'}, dimensions={0} | all-to-all | bytes 589824 | tf_op jit(solution)/shard_map/all_to_all | solution.py:120
  216.6 2.0 reshape.97
  218.6 1.8 copy.127
  221.5 2.2 fusion.44
  223.8 4.5 %all_to_all.90 = f32[2,2,3,64,200]{4,3,2,1,0:T(8,128)S(1)} all-to-all(f32[2,2,3,64,200]{4,3,2,1,0:T(8,128)S(1)} %broadcast_in_dim.91), channel_id=1, replica_groups=mesh['tc_0'=8,'tc_1'=4,'tc_2'=4,'pr'=2] {'pr'}, dimensions={0} | all-to-all | bytes 1228800 | tf_op jit(solution)/shard_map/all_to_all | solution.py:19
  228.4 1.3 fusion.47
  (82 shorter events, 23.0 us)
Async XLA Ops:
  0.6 227.7 %copy-start = (bf16[2,3,200,768]{3,2,1,0:T(8,128)(2,1)S(1)}, bf16[2,3,200,768]{3,2,1,0:T(8,128)(2,1)}, u32[]{:S(2)}) copy-start(bf16[2,3,200,768]{3,2,1,0:T(8,128)(2,1)} %param.17) | copy-start | bytes 5529604
  21.8 13.4 %copy-start.5 = (s32[3]{0:T(128)S(1)}, s32[3]{0:T(128)}, u32[]{:S(2)}) copy-start(s32[3]{0:T(128)} %param.12) | copy-start | bytes 40
  23.2 29.4 %copy-start.7 = (s32[1,2]{1,0:T(1,128)S(1)}, s32[1,2]{1,0:T(1,128)}, u32[]{:S(2)}) copy-start(s32[1,2]{1,0:T(1,128)} %param.15) | copy-start | bytes 28
  24.1 19.8 %all-to-all-start.1 = ((f32[32,1,384]{2,1,0:T(1,128)}), f32[32,1,384]{2,1,0:T(1,128)S(1)}, u32[]{:S(2)}, u32[]{:S(2)}) async-start(f32[32,1,384]{2,1,0:T(1,128)} %reshape.74), calls=%async_computation.1 | async-start | bytes 98304 | tf_op jit(solution)/shard_map/all_to_all | solution.py:51
  45.5 12.5 %all-to-all-start.2 = ((bf16[32,2,192]{2,1,0:T(2,128)(2,1)}), bf16[32,2,192]{2,1,0:T(2,128)(2,1)S(1)}, u32[]{:S(2)}, u32[]{:S(2)}) async-start(bf16[32,2,192]{2,1,0:T(2,128)(2,1)} %reshape.76), calls=%async_computation.2 | async-start | bytes 65536 | tf_op jit(solution)/shard_map/all_to_all | solution.py:19
  59.3 7.9 %all-to-all-start.3 = ((bf16[4,2,6144]{2,1,0:T(2,128)(2,1)}), bf16[4,2,6144]{2,1,0:T(2,128)(2,1)S(1)}, u32[]{:S(2)}, u32[]{:S(2)}) async-start(bf16[4,2,6144]{2,1,0:T(2,128)(2,1)} %reshape.78), calls=%async_computation.3 | async-start | bytes 196608 | tf_op jit(solution)/shard_map/all_to_all | solution.py:19
  62.6 5.2 %copy-start.3 = (f32[1,1536,32]{1,2,0:T(8,128)S(1)}, f32[1,1536,32]{1,2,0:T(8,128)}, u32[]{:S(2)}) copy-start(f32[1,1536,32]{1,2,0:T(8,128)} %param.10) | copy-start | bytes 589828
  69.8 3.3 %copy-start.1 = (f32[1536,32]{0,1:T(8,128)}, f32[1536,32]{0,1:T(8,128)S(1)}, u32[]{:S(2)}) copy-start(f32[1536,32]{0,1:T(8,128)S(1)} %fusion.6) | copy-start | bytes 589828
  102.2 12.5 %all-to-all-start.6 = ((bf16[32,2,192]{2,1,0:T(2,128)(2,1)}), bf16[32,2,192]{2,1,0:T(2,128)(2,1)S(1)}, u32[]{:S(2)}, u32[]{:S(2)}) async-start(bf16[32,2,192]{2,1,0:T(2,128)(2,1)} %reshape.84), calls=%async_computation.6 | async-start | bytes 65536 | tf_op jit(solution)/shard_map/all_to_all | solution.py:19
  115.9 7.9 %all-to-all-start.7 = ((bf16[4,2,6144]{2,1,0:T(2,128)(2,1)}), bf16[4,2,6144]{2,1,0:T(2,128)(2,1)S(1)}, u32[]{:S(2)}, u32[]{:S(2)}) async-start(bf16[4,2,6144]{2,1,0:T(2,128)(2,1)} %reshape.86), calls=%async_computation.7 | async-start | bytes 196608 | tf_op jit(solution)/shard_map/all_to_all | solution.py:19
  119.4 5.0 %copy-start.2 = (f32[1536,32]{0,1:T(8,128)S(1)}, f32[1536,32]{0,1:T(8,128)}, u32[]{:S(2)}) copy-start(f32[1536,32]{0,1:T(8,128)} %copy-done.1) | copy-start | bytes 589828
  174.8 8.2 %all-to-all-start.11 = ((bf16[4,2,6144]{2,1,0:T(2,128)(2,1)}), bf16[4,2,6144]{2,1,0:T(2,128)(2,1)S(1)}, u32[]{:S(2)}, u32[]{:S(2)}) async-start(bf16[4,2,6144]{2,1,0:T(2,128)(2,1)} %reshape.94), calls=%async_computation.11 | async-start | bytes 196608 | tf_op jit(solution)/shard_map/all_to_all | solution.py:19
  223.8 4.6 %copy-start.4 = (f32[2,64,768]{2,1,0:T(8,128)S(1)}, f32[2,64,768]{2,1,0:T(8,128)}, u32[]{:S(2)}) copy-start(f32[2,64,768]{2,1,0:T(8,128)} %param.19) | copy-start | bytes 1179652
  223.8 4.6 %copy-start.6 = (s32[2,3]{1,0:T(2,128)S(1)}, s32[2,3]{1,0:T(2,128)}, u32[]{:S(2)}) copy-start(s32[2,3]{1,0:T(2,128)} %param.18) | copy-start | bytes 76
where the time goes:
time: 231 us; the launch traced here: 230 us
  blocking collectives  84.4 us (37%)
  local copies, waits for them, and re-layouts  51.5 us (22%)
  waiting for transfers between devices  31.7 us (14%)
  starting transfers between devices  28.8 us (12%)
  matrix products  17.9 us (8%)
  other arithmetic  9.7 us (4%)
  between operations  5.64 us (2%)
    all_to_all x3, blocking collectives, sum_at_owner(): lax.all_to_all(pieces, axis, split_axis=0, concat_axis=0, tiled=True)  25.1 us
    all_to_all x2, blocking collectives, summed_rows(): return jnp.sum(lax.all_to_all(own, far, 0, 0, tiled=True), axis=0)  24.7 us
    all_to_all x5, waiting for transfers between devices, sent_to_all(): lax.all_to_all(jnp.broadcast_to(shard[None], (count, *shard.shape)), axis...  23.7 us
    unnamed x48, local copies, waits for them, and re-layouts  20.9 us
    all_to_all x1, blocking collectives, local(): lax.all_to_all(stacked, 'pr', split_axis=1, concat_axis=2, tiled=True)  18.6 us
    all_to_all x5, starting transfers between devices, sent_to_all(): lax.all_to_all(jnp.broadcast_to(shard[None], (count, *shard.shape)), axis...  17.8 us
    all_to_all x2, blocking collectives, sent_to_all(): lax.all_to_all(jnp.broadcast_to(shard[None], (count, *shard.shape)), axis...  16.1 us
    all_to_all x1, starting transfers between devices, summed_rows(): return jnp.sum(lax.all_to_all(own, far, 0, 0, tiled=True), axis=0)  11 us
  transfers between devices with their start and end apart: 6, of which 6 were waited for; matrix products, arithmetic and copies ran while one was open for 2% of the time, Pallas kernels for 0%

commit v1 on v0

--- a/solution.py
+++ b/solution.py
@@ -117,7 +117,15 @@
             change = jnp.dot(right_tile, factor, preferred_element_type=jnp.float32)
             pending = pending - jnp.where(active, change, 0.0)
     stacked = jnp.stack(solved)
-    columns = lax.all_to_all(stacked, "pr", split_axis=1, concat_axis=2, tiled=True)
+    columns = jnp.concatenate(
+        lax.all_to_all(
+            jnp.stack(jnp.split(stacked, lax.psum(1, "pr"), 1)),
+            axis_name="pr",
+            split_axis=0,
+            concat_axis=0,
+        ),
+        2,
+    )
     products = jnp.einsum(
         "sbq,fsrb->fsqr", columns, future_left, preferred_element_type=jnp.float32
     )

time: 231 us -> 210 us (0.909)
  local copies, waits for them, and re-layouts: 51.5 us -> 32 us
    another operation x2 -> x1, local copies, waits for them, and re-layouts: 8.25 us -> 0.02 us  [local(): jnp.stack(jnp.split(stacked, lax.psum(1, 'pr'), 1))]
    unnamed x48 -> x47, local copies, waits for them, and re-layouts: 20.9 us -> 13.5 us
    all_to_all x2 -> x1, local copies, waits for them, and re-layouts: 2.83 us -> 0.02 us  [local(): lax.all_to_all(jnp.stack(jnp.split(stacked, lax.psum(1, 'pr'), 1)), axis_...]
where the time goes in v1:
time: 210 us; the launch traced here: 209 us
  blocking collectives  83.8 us (40%)
  waiting for transfers between devices  32.2 us (15%)
  local copies, waits for them, and re-layouts  32 us (15%)
  starting transfers between devices  28.8 us (14%)
  matrix products  16.4 us (8%)
  other arithmetic  9.68 us (5%)
  between operations  5.68 us (3%)
    all_to_all x3, blocking collectives, sum_at_owner(): lax.all_to_all(pieces, axis, split_axis=0, concat_axis=0, tiled=True)  25.1 us
    all_to_all x2, blocking collectives, summed_rows(): return jnp.sum(lax.all_to_all(own, far, 0, 0, tiled=True), axis=0)  24.7 us
    all_to_all x5, waiting for transfers between devices, sent_to_all(): lax.all_to_all(jnp.broadcast_to(shard[None], (count, *shard.shape)), axis...  24.2 us
    all_to_all x1, blocking collectives, local(): lax.all_to_all(jnp.stack(jnp.split(stacked, lax.psum(1, 'pr'), 1)), axis_...  18 us
    all_to_all x5, starting transfers between devices, sent_to_all(): lax.all_to_all(jnp.broadcast_to(shard[None], (count, *shard.shape)), axis...  17.8 us
    all_to_all x2, blocking collectives, sent_to_all(): lax.all_to_all(jnp.broadcast_to(shard[None], (count, *shard.shape)), axis...  16.1 us
    unnamed x47, local copies, waits for them, and re-layouts  13.5 us
    all_to_all x1, starting transfers between devices, summed_rows(): return jnp.sum(lax.all_to_all(own, far, 0, 0, tiled=True), axis=0)  11 us
  transfers between devices with their start and end apart: 6, of which 6 were waited for; matrix products, arithmetic and copies ran while one was open for 2% of the time, Pallas kernels for 0%

profile of v1, /device:TPU:1, one launch (start us, length us, event | category | flops | bytes accessed | tf_op | source)
XLA Modules:
  0.0 208.7 jit_solution(14747441125403757951)
XLA Ops:
  0.7 1.4 fusion.79
  2.7 3.3 %fusion.15 = f32[1536,32]{0,1:T(8,128)S(1)} fusion(bf16[1,1536,1536]{2,1,0:T(8,128)(2,1)} %param.11, f32[1,1536,32]{1,2,0:T(8,128)} %param.10, pred[]{:T(512)S(6)} %eq.18), kind=kOutput, calls=%fused_computation.13 | convolution fusion | flops 151191552 | bytes 5111809 | tf_op jit(solution)/shard_map/dot_general | solution.py:96
  6.1 1.2 copy.79
  7.2 1.2 reshape_reshape.12
  8.4 1.3 copy.113
  9.8 1.5 reshape.80
  11.3 10.0 %all_to_all.70 = f32[4,1,12288]{2,1,0:T(1,128)S(1)} all-to-all(f32[4,1,12288]{2,1,0:T(1,128)S(1)} %reshape.80), channel_id=1, replica_groups=mesh['tc_0'=8,'tc_1'=4,'tc_2'=4,'pr'=2] {'tc_2'}, dimensions={0} | all-to-all | bytes 393216 | tf_op jit(solution)/shard_map/all_to_all | solution.py:44
  21.8 1.1 reduce
  23.4 0.8 reshape.82
  24.1 11.0 %all-to-all-start.1 = ((f32[32,1,384]{2,1,0:T(1,128)}), f32[32,1,384]{2,1,0:T(1,128)S(1)}, u32[]{:S(2)}, u32[]{:S(2)}) async-start(f32[32,1,384]{2,1,0:T(1,128)} %reshape.82), calls=%async_computation.1 | async-start | bytes 98304 | tf_op jit(solution)/shard_map/all_to_all | solution.py:51
  35.9 8.0 %all-to-all-done.1 = f32[32,1,384]{2,1,0:T(1,128)S(1)} async-done(((f32[32,1,384]{2,1,0:T(1,128)}), f32[32,1,384]{2,1,0:T(1,128)S(1)}, u32[]{:S(2)}, u32[]{:S(2)}) %all-to-all-start.1) | async-done | bytes 49184 | tf_op jit(solution)/shard_map/all_to_all | solution.py:51
  45.5 3.9 %all-to-all-start.2 = ((bf16[32,2,192]{2,1,0:T(2,128)(2,1)}), bf16[32,2,192]{2,1,0:T(2,128)(2,1)S(1)}, u32[]{:S(2)}, u32[]{:S(2)}) async-start(bf16[32,2,192]{2,1,0:T(2,128)(2,1)} %reshape.84), calls=%async_computation.2 | async-start | bytes 65536 | tf_op jit(solution)/shard_map/all_to_all | solution.py:19
  53.2 4.8 %all-to-all-done.2 = bf16[32,2,192]{2,1,0:T(2,128)(2,1)S(1)} async-done(((bf16[32,2,192]{2,1,0:T(2,128)(2,1)}), bf16[32,2,192]{2,1,0:T(2,128)(2,1)S(1)}, u32[]{:S(2)}, u32[]{:S(2)}) %all-to-all-start.2) | async-done | bytes 24608 | tf_op jit(solution)/shard_map/all_to_all | solution.py:19
  58.3 1.0 reshape.86
  59.3 3.3 %all-to-all-start.3 = ((bf16[4,2,6144]{2,1,0:T(2,128)(2,1)}), bf16[4,2,6144]{2,1,0:T(2,128)(2,1)S(1)}, u32[]{:S(2)}, u32[]{:S(2)}) async-start(bf16[4,2,6144]{2,1,0:T(2,128)(2,1)} %reshape.86), calls=%async_computation.3 | async-start | bytes 196608 | tf_op jit(solution)/shard_map/all_to_all | solution.py:19
  63.3 4.0 %all-to-all-done.3 = bf16[4,2,6144]{2,1,0:T(2,128)(2,1)S(1)} async-done(((bf16[4,2,6144]{2,1,0:T(2,128)(2,1)}), bf16[4,2,6144]{2,1,0:T(2,128)(2,1)S(1)}, u32[]{:S(2)}, u32[]{:S(2)}) %all-to-all-start.3) | async-done | bytes 98336 | tf_op jit(solution)/shard_map/all_to_all | solution.py:19
  67.9 1.9 fusion.6
  69.8 3.3 %fusion.27 = f32[1536,32]{0,1:T(8,128)S(1)} fusion(bf16[1,1536,1536]{2,1,0:T(8,128)(2,1)} %param.11, f32[1536,32]{0,1:T(8,128)S(1)} %fusion.6, pred[]{:T(512)S(6)} %eq.19), kind=kOutput, calls=%fused_computation.17 | convolution fusion | flops 151191552 | bytes 5111809 | tf_op jit(solution)/shard_map/dot_general | solution.py:96
  73.1 1.2 copy.84
  74.3 1.2 reshape_reshape.13
  75.5 1.3 copy.112
  76.8 1.5 reshape.88
  78.3 7.5 %all_to_all.71 = f32[4,1,12288]{2,1,0:T(1,128)S(1)} all-to-all(f32[4,1,12288]{2,1,0:T(1,128)S(1)} %reshape.88), channel_id=1, replica_groups=mesh['tc_0'=8,'tc_1'=4,'tc_2'=4,'pr'=2] {'tc_2'}, dimensions={0} | all-to-all | bytes 393216 | tf_op jit(solution)/shard_map/all_to_all | solution.py:44
  85.9 1.1 reduce.2
  87.6 12.9 %all_to_all.72 = f32[32,1,384]{2,1,0:T(1,128)S(1)} all-to-all(f32[32,1,384]{2,1,0:T(1,128)S(1)} %reshape.90), channel_id=1, replica_groups=mesh['tc_0'=8,'tc_1'=4,'tc_2'=4,'pr'=2] {'tc_0','tc_1'}, dimensions={0} | all-to-all | bytes 98304 | tf_op jit(solution)/shard_map/all_to_all | solution.py:51
  102.2 3.9 %all-to-all-start.6 = ((bf16[32,2,192]{2,1,0:T(2,128)(2,1)}), bf16[32,2,192]{2,1,0:T(2,128)(2,1)S(1)}, u32[]{:S(2)}, u32[]{:S(2)}) async-start(bf16[32,2,192]{2,1,0:T(2,128)(2,1)} %reshape.92), calls=%async_computation.6 | async-start | bytes 65536 | tf_op jit(solution)/shard_map/all_to_all | solution.py:19
  107.2 7.4 %all-to-all-done.6 = bf16[32,2,192]{2,1,0:T(2,128)(2,1)S(1)} async-done(((bf16[32,2,192]{2,1,0:T(2,128)(2,1)}), bf16[32,2,192]{2,1,0:T(2,128)(2,1)S(1)}, u32[]{:S(2)}, u32[]{:S(2)}) %all-to-all-start.6) | async-done | bytes 24608 | tf_op jit(solution)/shard_map/all_to_all | solution.py:19
  114.9 1.0 reshape.94
  116.0 3.5 %all-to-all-start.7 = ((bf16[4,2,6144]{2,1,0:T(2,128)(2,1)}), bf16[4,2,6144]{2,1,0:T(2,128)(2,1)S(1)}, u32[]{:S(2)}, u32[]{:S(2)}) async-start(bf16[4,2,6144]{2,1,0:T(2,128)(2,1)} %reshape.94), calls=%async_computation.7 | async-start | bytes 196608 | tf_op jit(solution)/shard_map/all_to_all | solution.py:19
  120.1 3.8 %all-to-all-done.7 = bf16[4,2,6144]{2,1,0:T(2,128)(2,1)S(1)} async-done(((bf16[4,2,6144]{2,1,0:T(2,128)(2,1)}), bf16[4,2,6144]{2,1,0:T(2,128)(2,1)S(1)}, u32[]{:S(2)}, u32[]{:S(2)}) %all-to-all-start.7) | async-done | bytes 98336 | tf_op jit(solution)/shard_map/all_to_all | solution.py:19
  124.5 2.6 %fusion.8 = bf16[1536,32]{0,1:T(8,128)(2,1)} fusion(f32[1536,32]{0,1:T(8,128)S(1)} %copy-done.3, bf16[1536,32]{1,0:T(8,128)(2,1)S(1)} %convert_element_type.112, bf16[1,2,1536,200]{2,3,1,0:T(8,128)(2,1)} %param.13, s32[]{:T(128)S(6)} %min.8, bf16[1,2,1536,200]{2,3,1,0:T(8,128)(2,1)} %param.14, pred[]{:T(512)S(6)} %and.10, ...), kind=kOutput, calls=%fused_computation.10 | convolution fusion | flops 39481856 | bytes 1623752 | tf_op jit(solution)/shard_map/dot_general | solution.py:117
  127.1 3.3 %fusion.39 = f32[1536,32]{0,1:T(8,128)S(1)} fusion(bf16[1536,32]{0,1:T(8,128)(2,1)} %fusion.8, bf16[1,1536,1536]{2,1,0:T(8,128)(2,1)} %param.11, pred[]{:T(512)S(6)} %eq.15), kind=kOutput, calls=%fused_computation.21 | convolution fusion | flops 151142400 | bytes 5013505 | tf_op jit(solution)/shard_map/dot_general | solution.py:96
  130.4 1.2 copy.89
  131.6 2.2 %reshape_reshape.14 = f32[32,4,12,32]{3,2,1,0:T(8,128)} reshape(f32[1536,32]{1,0:T(8,128)} %copy.89) | data formatting | bytes 393216 | tf_op jit(solution)/shard_map/reshape;reshape | solution.py:38
  133.8 2.6 %copy.111 = f32[4,32,12,32]{3,1,2,0:T(8,128)} copy(f32[4,32,12,32]{3,2,0,1:T(8,128)} %bitcast.124) | data formatting | bytes 393216 | tf_op jit(solution)/shard_map/transpose | solution.py:39
  136.4 1.5 reshape.96
  137.9 7.5 %all_to_all.73 = f32[4,1,12288]{2,1,0:T(1,128)S(1)} all-to-all(f32[4,1,12288]{2,1,0:T(1,128)S(1)} %reshape.96), channel_id=1, replica_groups=mesh['tc_0'=8,'tc_1'=4,'tc_2'=4,'pr'=2] {'tc_2'}, dimensions={0} | all-to-all | bytes 393216 | tf_op jit(solution)/shard_map/all_to_all | solution.py:44
  145.4 1.1 reduce.4
  146.5 1.2 reshape.97
  147.7 1.2 bitcast_reduce_fusion
  149.2 11.7 %all_to_all.74 = f32[32,1,384]{2,1,0:T(1,128)S(1)} all-to-all(f32[32,1,384]{2,1,0:T(1,128)S(1)} %reshape.98), channel_id=1, replica_groups=mesh['tc_0'=8,'tc_1'=4,'tc_2'=4,'pr'=2] {'tc_0','tc_1'}, dimensions={0} | all-to-all | bytes 98304 | tf_op jit(solution)/shard_map/all_to_all | solution.py:51
  161.9 11.6 %all_to_all.75 = bf16[32,2,192]{2,1,0:T(2,128)(2,1)S(1)} all-to-all(bf16[32,2,192]{2,1,0:T(2,128)(2,1)S(1)} %reshape.100), channel_id=1, replica_groups=mesh['tc_0'=8,'tc_1'=4,'tc_2'=4,'pr'=2] {'tc_0','tc_1'}, dimensions={0} | all-to-all | bytes 49152 | tf_op jit(solution)/shard_map/all_to_all | solution.py:19
  173.7 1.1 reshape.102
  174.8 3.3 %all-to-all-start.11 = ((bf16[4,2,6144]{2,1,0:T(2,128)(2,1)}), bf16[4,2,6144]{2,1,0:T(2,128)(2,1)S(1)}, u32[]{:S(2)}, u32[]{:S(2)}) async-start(bf16[4,2,6144]{2,1,0:T(2,128)(2,1)} %reshape.102), calls=%async_computation.11 | async-start | bytes 196608 | tf_op jit(solution)/shard_map/all_to_all | solution.py:19
  178.8 4.2 %all-to-all-done.11 = bf16[4,2,6144]{2,1,0:T(2,128)(2,1)S(1)} async-done(((bf16[4,2,6144]{2,1,0:T(2,128)(2,1)}), bf16[4,2,6144]{2,1,0:T(2,128)(2,1)S(1)}, u32[]{:S(2)}, u32[]{:S(2)}) %all-to-all-start.11) | async-done | bytes 98336 | tf_op jit(solution)/shard_map/all_to_all | solution.py:19
  183.9 18.0 %all_to_all.76 = bf16[2,3,768,32]{2,3,1,0:T(8,128)(2,1)S(1)} all-to-all(bf16[2,3,768,32]{2,3,1,0:T(8,128)(2,1)S(1)} %pad_maximum_fusion.1), channel_id=1, replica_groups=mesh['tc_0'=8,'tc_1'=4,'tc_2'=4,'pr'=2] {'pr'}, dimensions={0} | all-to-all | bytes 589824 | tf_op jit(solution)/shard_map/all_to_all | solution.py:121
  202.8 4.5 %all_to_all.77 = f32[2,2,3,64,200]{4,3,2,1,0:T(8,128)S(1)} all-to-all(f32[2,2,3,64,200]{4,3,2,1,0:T(8,128)S(1)} %broadcast_in_dim.91), channel_id=1, replica_groups=mesh['tc_0'=8,'tc_1'=4,'tc_2'=4,'pr'=2] {'pr'}, dimensions={0} | all-to-all | bytes 1228800 | tf_op jit(solution)/shard_map/all_to_all | solution.py:19
  207.3 1.3 fusion.47
  (84 shorter events, 13.5 us)
Async XLA Ops:
  0.6 206.7 %copy-start = (bf16[2,3,200,768]{3,2,1,0:T(8,128)(2,1)S(1)}, bf16[2,3,200,768]{3,2,1,0:T(8,128)(2,1)}, u32[]{:S(2)}) copy-start(bf16[2,3,200,768]{3,2,1,0:T(8,128)(2,1)} %param.17) | copy-start | bytes 5529604
  11.3 23.9 %copy-start.7 = (s32[3]{0:T(128)S(1)}, s32[3]{0:T(128)}, u32[]{:S(2)}) copy-start(s32[3]{0:T(128)} %param.12) | copy-start | bytes 40
  22.9 29.7 %copy-start.9 = (s32[1,2]{1,0:T(1,128)S(1)}, s32[1,2]{1,0:T(1,128)}, u32[]{:S(2)}) copy-start(s32[1,2]{1,0:T(1,128)} %param.15) | copy-start | bytes 28
  24.1 19.8 %all-to-all-start.1 = ((f32[32,1,384]{2,1,0:T(1,128)}), f32[32,1,384]{2,1,0:T(1,128)S(1)}, u32[]{:S(2)}, u32[]{:S(2)}) async-start(f32[32,1,384]{2,1,0:T(1,128)} %reshape.82), calls=%async_computation.1 | async-start | bytes 98304 | tf_op jit(solution)/shard_map/all_to_all | solution.py:51
  45.5 12.5 %all-to-all-start.2 = ((bf16[32,2,192]{2,1,0:T(2,128)(2,1)}), bf16[32,2,192]{2,1,0:T(2,128)(2,1)S(1)}, u32[]{:S(2)}, u32[]{:S(2)}) async-start(bf16[32,2,192]{2,1,0:T(2,128)(2,1)} %reshape.84), calls=%async_computation.2 | async-start | bytes 65536 | tf_op jit(solution)/shard_map/all_to_all | solution.py:19
  58.3 9.6 %copy-start.5 = (f32[1,1536,32]{1,2,0:T(8,128)S(1)}, f32[1,1536,32]{1,2,0:T(8,128)}, u32[]{:S(2)}) copy-start(f32[1,1536,32]{1,2,0:T(8,128)} %param.10) | copy-start | bytes 589828
  59.3 7.9 %all-to-all-start.3 = ((bf16[4,2,6144]{2,1,0:T(2,128)(2,1)}), bf16[4,2,6144]{2,1,0:T(2,128)(2,1)S(1)}, u32[]{:S(2)}, u32[]{:S(2)}) async-start(bf16[4,2,6144]{2,1,0:T(2,128)(2,1)} %reshape.86), calls=%async_computation.3 | async-start | bytes 196608 | tf_op jit(solution)/shard_map/all_to_all | solution.py:19
  69.8 3.3 %copy-start.2 = (f32[1536,32]{0,1:T(8,128)}, f32[1536,32]{0,1:T(8,128)S(1)}, u32[]{:S(2)}) copy-start(f32[1536,32]{0,1:T(8,128)S(1)} %fusion.6) | copy-start | bytes 589828
  102.2 12.5 %all-to-all-start.6 = ((bf16[32,2,192]{2,1,0:T(2,128)(2,1)}), bf16[32,2,192]{2,1,0:T(2,128)(2,1)S(1)}, u32[]{:S(2)}, u32[]{:S(2)}) async-start(bf16[32,2,192]{2,1,0:T(2,128)(2,1)} %reshape.92), calls=%async_computation.6 | async-start | bytes 65536 | tf_op jit(solution)/shard_map/all_to_all | solution.py:19
  114.9 9.6 %copy-start.3 = (f32[1536,32]{0,1:T(8,128)S(1)}, f32[1536,32]{0,1:T(8,128)}, u32[]{:S(2)}) copy-start(f32[1536,32]{0,1:T(8,128)} %copy-done.2) | copy-start | bytes 589828
  116.0 7.9 %all-to-all-start.7 = ((bf16[4,2,6144]{2,1,0:T(2,128)(2,1)}), bf16[4,2,6144]{2,1,0:T(2,128)(2,1)S(1)}, u32[]{:S(2)}, u32[]{:S(2)}) async-start(bf16[4,2,6144]{2,1,0:T(2,128)(2,1)} %reshape.94), calls=%async_computation.7 | async-start | bytes 196608 | tf_op jit(solution)/shard_map/all_to_all | solution.py:19
  174.8 8.2 %all-to-all-start.11 = ((bf16[4,2,6144]{2,1,0:T(2,128)(2,1)}), bf16[4,2,6144]{2,1,0:T(2,128)(2,1)S(1)}, u32[]{:S(2)}, u32[]{:S(2)}) async-start(bf16[4,2,6144]{2,1,0:T(2,128)(2,1)} %reshape.102), calls=%async_computation.11 | async-start | bytes 196608 | tf_op jit(solution)/shard_map/all_to_all | solution.py:19
  183.8 18.1 %copy-start.1 = (bf16[2,3,200,768]{3,2,1,0:T(8,128)(2,1)S(1)}, bf16[2,3,200,768]{3,2,1,0:T(8,128)(2,1)}, u32[]{:S(2)}) copy-start(bf16[2,3,200,768]{3,2,1,0:T(8,128)(2,1)} %param.16) | copy-start | bytes 5529604
  183.8 18.8 %copy-start.4 = (bf16[3,1536,32]{1,2,0:T(8,128)(2,1)}, bf16[3,1536,32]{1,2,0:T(8,128)(2,1)S(1)}, u32[]{:S(2)}) copy-start(bf16[3,1536,32]{1,2,0:T(8,128)(2,1)S(1)} %pad_maximum_fusion) | copy-start | bytes 884740
  202.7 4.7 %copy-start.6 = (f32[2,64,768]{2,1,0:T(8,128)S(1)}, f32[2,64,768]{2,1,0:T(8,128)}, u32[]{:S(2)}) copy-start(f32[2,64,768]{2,1,0:T(8,128)} %param.19) | copy-start | bytes 1179652
  202.7 4.7 %copy-start.8 = (s32[2,3]{1,0:T(2,128)S(1)}, s32[2,3]{1,0:T(2,128)}, u32[]{:S(2)}) copy-start(s32[2,3]{1,0:T(2,128)} %param.18) | copy-start | bytes 76
